TPU v7x, 32 devices: a whole 2x2x4 slice. The times are simulated.
32 devices in a mesh: req: 8 (over z, x), grp: 4 (over y, core).
Axes of the slice: x: 2, y: 2, z: 4, core: 2. Of those that a mesh axis runs over, the one named last changes fastest.
Arguments:
- hidden: bfloat16 [256, 16, 1024], P(('grp', 'req')), parts along dimension 0, may hold values from -6 to 6
- norm_gain: float32 [1024], replicated, may hold values from 0.1 to 1.9
- in_weight: bfloat16 [1024, 4096], replicated, may hold values from -0.1875 to 0.1875
- conv_weight: float32 [4, 2048], P(None, 'req'), may hold values from -3 to 3
- conv_bias: float32 [2048], P('req'), may hold values from -3 to 3
- x_weight: bfloat16 [2048, 160], P('req'), may hold values from -0.125 to 0.125
- step_weight: bfloat16 [128, 2048], P(None, 'req'), may hold values from -0.5 to 0.5
- step_bias: float32 [2048], P('req'), may hold values from -5 to -1
- log_decay: float32 [16, 2048], P(None, 'req'), may hold values from -0.7 to 2.8
- skip_gain: float32 [2048], P('req'), may hold values from 0.5 to 1.5
- out_weight: bfloat16 [2048, 1024], replicated, may hold values from -0.125 to 0.125
- old_states: float32 [256, 16, 2048], P(('grp', 'req')), parts along dimension 0, may hold values from -3 to 3
- old_edges: bfloat16 [256, 3, 2048], P(('grp', 'req')), parts along dimension 0, may hold values from -6 to 6
- anchor: int32 [256], P('grp'), parts along dimension 0, may hold values from 0 to 63, each once
- fresh_flag: int32 [256], P('grp'), parts along dimension 0, may hold values 0 or 1
- accepted: int32 [256], P('grp'), parts along dimension 0, may hold values from 1 to 16
- request_ages: int32 [256], P('grp'), parts along dimension 0, may hold values from 0 to 7
Outputs:
- layer_out: bfloat16 [256, 16, 1024], P(('grp', 'req')), parts along dimension 0
- new_states: float32 [256, 16, 2048], P(('grp', 'req')), parts along dimension 0
There are 4 independent parts, one for each index of `grp`. A program takes and returns all parts, laid end to end along the dimension named above; an argument that names none is the same for every part. Nothing has to cross between parts.
Inputs may be any that keep to these rules, and one draw needn't show every extreme that they name: Every old slot is the anchor of exactly one request.
All inputs are finite; a program needn't handle non-finite values.
Results may differ from a plain program's by a relative error of at most 0.0091.
Values may be sent and summed in bfloat16 or wider, within the bound.
No kernel may reach another device: no remote copies, remote signals or barrier semaphores. Data moves between devices by JAX's collectives and lax.ppermute only.
A program may use at most 128 MiB of HBM per device.

v0:
```python
import jax
import jax.numpy as jnp
from jax import lax
from jax.sharding import PartitionSpec as P

EPS = 1e-05


def rms_normed(values_in, norm_gain):
    values = values_in.astype(jnp.float32)
    factor = lax.rsqrt(jnp.mean(values * values, axis=-1, keepdims=True) + EPS)
    return (values * factor * norm_gain).astype(jnp.bfloat16)


def on_device(
    hidden,
    norm_gain,
    in_weight,
    conv_weight,
    conv_bias,
    x_weight,
    step_weight,
    step_bias,
    log_decay,
    skip_gain,
    out_weight,
    old_states,
    old_edges,
    anchor,
    fresh_flag,
    accepted,
    request_ages,
):
    local_reqs, draft_len, width = hidden.shape
    inner_width = out_weight.shape[0]
    channels = conv_weight.shape[1]
    state_size = log_decay.shape[0]
    low_rank = step_weight.shape[0]
    span = old_edges.shape[1]
    state_lead = jnp.swapaxes(old_states, 0, 1)
    edge_lead = jnp.swapaxes(old_edges.astype(jnp.float32), 0, 1)
    moved_states, moved_edges = (
        lax.all_to_all(state_lead, "req", split_axis=2, concat_axis=1, tiled=True),
        lax.all_to_all(edge_lead, "req", split_axis=2, concat_axis=1, tiled=True),
    )
    token_major = jnp.swapaxes(hidden, 0, 1).reshape(draft_len * local_reqs, width)
    normed = rms_normed(token_major, norm_gain)
    projected = jnp.dot(normed, in_weight, preferred_element_type=jnp.float32).astype(jnp.bfloat16)
    projected = jnp.moveaxis(projected.reshape(draft_len, local_reqs, 2, inner_width), 2, 0)
    grouped = lax.all_to_all(projected, "req", split_axis=3, concat_axis=2, tiled=True)
    all_reqs = grouped.shape[2]
    inner_part = grouped[0]
    gate_part = grouped[1]
    keep_state = (1 - fresh_flag).astype(jnp.float32)
    start_state = jnp.take(moved_states, anchor, axis=1) * keep_state[None, :, None]
    edges = jnp.take(moved_edges, anchor, axis=1)
    distance = span - jnp.arange(span, dtype=jnp.int32)
    usable = (distance[:, None] <= request_ages[None, :]) & (fresh_flag[None, :] == 0)
    history = jnp.where(usable[:, :, None], edges, jnp.zeros((), jnp.float32))
    sequence = jnp.concatenate([history, inner_part.astype(jnp.float32)], axis=0)
    running = conv_bias + conv_weight[0] * sequence[0:draft_len]
    for offset in range(1, conv_weight.shape[0]):
        running = running + conv_weight[offset] * sequence[offset : offset + draft_len]
    conv_out = jax.nn.silu(running).astype(jnp.bfloat16)
    conv_rows = conv_out.reshape(draft_len * all_reqs, channels)
    partial_value = jnp.dot(conv_rows, x_weight, preferred_element_type=jnp.float32)
    mixed_rows = lax.psum(partial_value, "req").astype(jnp.bfloat16)
    flat = all_reqs * channels
    step_sizes = jax.nn.softplus(
        jnp.dot(mixed_rows[:, :low_rank], step_weight, preferred_element_type=jnp.float32)
        + step_bias
    )
    step_sizes = step_sizes.reshape(draft_len, flat)
    coeffs = (
        mixed_rows[:, low_rank:].astype(jnp.float32).reshape(draft_len, all_reqs, 2 * state_size)
    )
    b_coeff = coeffs[:, :, :state_size]
    c_coeff = coeffs[:, :, state_size:]
    inputs = conv_out.astype(jnp.float32)
    flat_inputs = inputs.reshape(draft_len, flat)
    decay = jnp.broadcast_to(
        (-jnp.exp(log_decay))[:, None, :], (state_size, all_reqs, channels)
    ).reshape(state_size, flat)
    start_flat = start_state.reshape(state_size, flat)

    def spread(per_token):
        return jnp.broadcast_to(
            jnp.swapaxes(per_token, 0, 1)[:, :, None], (state_size, all_reqs, channels)
        ).reshape(state_size, flat)

    def advance(carried, sliced):
        current, chosen = carried
        step_delta, step_b, step_c, step_input, step_index = sliced
        factor = jnp.exp(step_delta[None, :] * decay)
        current = factor * current + (step_delta * step_input)[None, :] * spread(step_b)
        result = jnp.sum(spread(step_c) * current, axis=0)
        picked = jnp.broadcast_to(
            (accepted == step_index + 1)[:, None], (all_reqs, channels)
        ).reshape(flat)
        chosen = jnp.where(picked[None, :], current, chosen)
        return ((current, chosen), result)

    sliced = (step_sizes, b_coeff, c_coeff, flat_inputs, jnp.arange(draft_len, dtype=jnp.int32))
    (final_state, chosen), outputs = lax.scan(advance, (start_flat, start_flat), sliced)
    outputs = outputs.reshape(draft_len, all_reqs, channels)
    gated_rows = (
        (outputs + skip_gain * inputs) * jax.nn.silu(gate_part.astype(jnp.float32))
    ).astype(jnp.bfloat16)
    returned = lax.all_to_all(gated_rows, "req", split_axis=1, concat_axis=2, tiled=True)
    layer_out = jnp.dot(
        returned.reshape(draft_len * local_reqs, inner_width),
        out_weight,
        preferred_element_type=jnp.float32,
    ).astype(jnp.bfloat16)
    layer_out = jnp.swapaxes(layer_out.reshape(draft_len, local_reqs, width), 0, 1)
    owned = lax.all_to_all(
        chosen.reshape(state_size, all_reqs, channels),
        "req",
        split_axis=1,
        concat_axis=2,
        tiled=True,
    )
    return (layer_out, jnp.swapaxes(owned, 0, 1))


def solution(mesh):
    return jax.shard_map(
        on_device,
        mesh=mesh,
        in_specs=(
            P(("grp", "req"), None, None),
            P(),
            P(),
            P(None, "req"),
            P("req"),
            P("req", None),
            P(None, "req"),
            P("req"),
            P(None, "req"),
            P("req"),
            P(),
            P(("grp", "req"), None, None),
            P(("grp", "req"), None, None),
            P("grp"),
            P("grp"),
            P("grp"),
            P("grp"),
        ),
        out_specs=(P(("grp", "req"), None, None), P(("grp", "req"), None, None)),
        check_vma=False,
    )
```

profile of v0, /device:TPU:0, one launch (start us, length us, event | category | flops | bytes accessed | tf_op | source)
XLA Modules:
  0.0 369.8 jit_solution(14479661632174473123)
XLA Ops:
  0.7 4.0 %copy.100 = f32[8,3,2048]{0,1,2:T(4,128)} copy(bf16[8,3,2048]{2,0,1:T(8,128)(2,1)} %param.31) | data formatting | bytes 294912 | tf_op jit(solution)/shard_map/transpose | solution.py:41
  4.7 3.9 %bitcast_bitcast_fusion.2 = f32[2048,3,8]{2,1,0:T(4,128)} fusion(f32[8,3,2048]{0,1,2:T(4,128)} %copy.100), kind=kLoop, calls=%fused_computation.72 | loop fusion | bytes 393216
  8.6 5.1 %reshape.188 = f32[8,1,6144]{2,1,0:T(1,128)} reshape(f32[2048,3,8]{2,1,0:T(4,128)} %bitcast_bitcast_fusion.2) | data formatting | bytes 393216
  13.7 7.3 %all-to-all-start.1 = ((f32[8,1,6144]{2,1,0:T(1,128)}), f32[8,1,6144]{2,1,0:T(1,128)S(1)}, u32[]{:S(2)}, u32[]{:S(2)}) async-start(f32[8,1,6144]{2,1,0:T(1,128)} %reshape.188), calls=%async_computation.1 | async-start | bytes 393216 | tf_op jit(solution)/shard_map/all_to_all | solution.py:44
  20.9 4.7 %copy.94 = f32[8,16,2048]{1,0,2:T(8,128)} copy(f32[8,16,2048]{2,1,0:T(8,128)S(1)} %copy-done.3) | data formatting | bytes 2097152 | tf_op args[11]
  26.0 4.8 %convolution_convert_fusion = bf16[128,4096]{1,0:T(8,128)(2,1)S(1)} fusion(bf16[1024,4096]{1,0:T(8,128)(2,1)} %param.21, f32[1024]{0:T(1024)S(1)} %copy-done.4, f32[128]{0:T(128)S(1)} %rsqrt.12, bf16[8,16,1024]{2,1,0:T(8,128)(2,1)S(1)} %copy-done.2), kind=kOutput, calls=%fused_computation.11 | convolution fusion | flops 1074790400 | bytes 9703936 | tf_op jit(solution)/shard_map/dot_general | solution.py:48
  30.8 8.9 %copy.103 = bf16[16,8,2,2048]{0,1,2,3:T(8,128)(2,1)} copy(bf16[16,8,2,2048]{3,1,2,0:T(8,128)(2,1)S(1)} %bitcast.169) | data formatting | bytes 2097152 | tf_op jit(solution)/shard_map/reshape | solution.py:49
  39.6 7.5 %bitcast_bitcast_fusion = bf16[2048,2,8,16]{3,2,1,0:T(8,128)(2,1)} fusion(bf16[16,8,2,2048]{0,1,2,3:T(8,128)(2,1)} %copy.103), kind=kLoop, calls=%fused_computation.70 | loop fusion | bytes 2097152
  47.1 5.8 %bitcast_bitcast_fusion.1 = f32[2048,8,16]{2,1,0:T(8,128)} fusion(f32[8,16,2048]{1,0,2:T(8,128)} %copy.94), kind=kLoop, calls=%fused_computation.71 | loop fusion | bytes 2097152
  52.9 8.1 %reshape.184 = f32[8,1,32768]{2,1,0:T(1,128)} reshape(f32[2048,8,16]{2,1,0:T(8,128)} %bitcast_bitcast_fusion.1) | data formatting | bytes 2097152
  61.1 6.0 %all-to-all-start = ((f32[8,1,32768]{2,1,0:T(1,128)}), f32[8,1,32768]{2,1,0:T(1,128)S(1)}, u32[]{:S(2)}, u32[]{:S(2)}) async-start(f32[8,1,32768]{2,1,0:T(1,128)} %reshape.184), calls=%async_computation | async-start | bytes 2097152 | tf_op jit(solution)/shard_map/all_to_all | solution.py:43
  67.3 11.3 %reshape.186 = bf16[8,2,32768]{2,1,0:T(2,128)(2,1)} reshape(bf16[2048,2,8,16]{3,2,1,0:T(8,128)(2,1)} %bitcast_bitcast_fusion) | data formatting | bytes 2097152
  80.5 4.7 %reshape.189 = f32[2048,3,8]{2,1,0:T(4,128)} reshape(f32[8,6144]{1,0:T(8,128)S(1)} %reduce.3) | data formatting | bytes 393216
  85.2 3.5 copy.101
  89.6 2.9 all-to-all-done
  92.5 3.7 %all-to-all-start.2 = ((bf16[8,2,32768]{2,1,0:T(2,128)(2,1)}), bf16[8,2,32768]{2,1,0:T(2,128)(2,1)S(1)}, u32[]{:S(2)}, u32[]{:S(2)}) async-start(bf16[8,2,32768]{2,1,0:T(2,128)(2,1)} %reshape.186), calls=%async_computation.2 | async-start | bytes 2097152 | tf_op jit(solution)/shard_map/all_to_all | solution.py:50
  96.3 3.1 reduce.2
  99.4 6.1 %reshape.185 = f32[2048,8,16]{2,1,0:T(8,128)} reshape(f32[8,32768]{1,0:T(8,128)S(1)} %reduce.2) | data formatting | bytes 2097152
  105.5 5.4 %copy.96 = f32[16,8,8,256]{3,2,1,0:T(8,128)S(1)} copy(f32[16,8,8,256]{0,2,3,1:T(8,128)} %bitcast.155) | data formatting | bytes 2097152 | tf_op jit(solution)/shard_map/all_to_all | solution.py:43
  112.4 9.5 %all-to-all-done.2 = bf16[8,2,32768]{2,1,0:T(2,128)(2,1)S(1)} async-done(((bf16[8,2,32768]{2,1,0:T(2,128)(2,1)}), bf16[8,2,32768]{2,1,0:T(2,128)(2,1)S(1)}, u32[]{:S(2)}, u32[]{:S(2)}) %all-to-all-start.2) | async-done | bytes 1048608 | tf_op jit(solution)/shard_map/all_to_all | solution.py:50
  121.9 7.6 %reshape.187 = bf16[2048,2,8,16]{3,2,1,0:T(8,128)(2,1)} reshape(bf16[8,2,32768]{2,1,0:T(2,128)(2,1)S(1)} %all-to-all-done.2) | data formatting | bytes 2097152
  129.5 8.9 %copy.104 = bf16[2,16,8,8,256]{4,2,3,1,0:T(8,128)(2,1)S(1)} copy(bf16[2,16,8,8,256]{1,2,0,4,3:T(8,128)(2,1)} %bitcast.156) | data formatting | bytes 2097152 | tf_op jit(solution)/shard_map/all_to_all | solution.py:50
  140.2 43.6 %all-reduce.1 = bf16[1024,160]{0,1:T(8,128)(2,1)} all-reduce(f32[1024,160]{0,1:T(8,128)S(1)} %fusion.29), channel_id=1, replica_groups=mesh['req'=8,'grp'=4] {'req'}, use_global_device_ids=true, to_apply=%region_1.2 | all-reduce | flops 163840 | bytes 983040 | tf_op jit(solution)/shard_map/psum | solution.py:67
  184.7 2.7 compare_select_fusion
  187.4 2.4 reshape.145
  191.2 132.7 %while.15 = (s32[]{:T(128)}, f32[16,16384]{1,0:T(8,128)S(1)}, f32[16,16384]{1,0:T(8,128)S(1)}, f32[16,16384]{1,0:T(8,128)}, f32[16,16384]{1,0:T(8,128)}, /*index...) while((s32[]{:T(128)}, f32[16,16384]{1,0:T(8,128)S(1)}, ...), condition=%wide.region_4.5_spmd.clone, body=%wide.region_2.4_spmd.clone.sunk | while | flops 1835075 | bytes 18522676 | solution.py:104
  192.9 1.3 constant_dynamic-slice_fusion.6
  197.6 1.9 dynamic_update_slice.6
  201.2 1.3 constant_dynamic-slice_fusion.6
  205.9 1.9 dynamic_update_slice.6
  209.5 1.3 constant_dynamic-slice_fusion.6
  214.2 1.9 dynamic_update_slice.6
  217.8 1.3 constant_dynamic-slice_fusion.6
  222.5 1.9 dynamic_update_slice.6
  226.1 1.3 constant_dynamic-slice_fusion.6
  230.7 1.9 dynamic_update_slice.6
  234.3 1.3 constant_dynamic-slice_fusion.6
  239.0 1.9 dynamic_update_slice.6
  242.6 1.3 constant_dynamic-slice_fusion.6
  247.3 1.9 dynamic_update_slice.6
  250.9 1.3 constant_dynamic-slice_fusion.6
  255.6 1.9 dynamic_update_slice.6
  259.2 1.3 constant_dynamic-slice_fusion.6
  263.9 1.9 dynamic_update_slice.6
  267.5 1.3 constant_dynamic-slice_fusion.6
  272.2 1.9 dynamic_update_slice.6
  275.8 1.3 constant_dynamic-slice_fusion.6
  280.5 1.9 dynamic_update_slice.6
  288.8 1.9 dynamic_update_slice.6
  292.4 1.3 constant_dynamic-slice_fusion.6
  297.1 1.9 dynamic_update_slice.6
  300.7 1.3 constant_dynamic-slice_fusion.6
  305.4 1.9 dynamic_update_slice.6
  313.7 1.9 dynamic_update_slice.6
  317.3 1.3 constant_dynamic-slice_fusion.6
  322.0 1.9 dynamic_update_slice.6
  323.9 1.5 copy.127
  325.5 1.5 fusion.16
  328.1 3.5 all-to-all-start.3
  332.7 9.4 %all-to-all-done.3 = bf16[16,64,256]{2,0,1:T(8,128)(2,1)S(1)} async-done(((bf16[16,64,256]{2,0,1:T(8,128)(2,1)}), bf16[16,64,256]{2,0,1:T(8,128)(2,1)S(1)}, u32[]{:S(2)}, u32[]{:S(2)}) %all-to-all-start.3) | async-done | bytes 524320 | tf_op jit(solution)/shard_map/all_to_all | solution.py:109
  342.1 9.1 %all-to-all-start.4 = ((f32[16,64,256]{2,0,1:T(8,128)}), f32[16,64,256]{2,0,1:T(8,128)S(1)}, u32[]{:S(2)}, u32[]{:S(2)}) async-start(f32[16,64,256]{2,0,1:T(8,128)} %bitcast.121), calls=%async_computation.4 | async-start | bytes 2097152 | tf_op jit(solution)/shard_map/all_to_all | solution.py:116
  351.6 2.9 fusion.2
  355.4 12.2 %all-to-all-done.4 = f32[16,64,256]{2,0,1:T(8,128)S(1)} async-done(((f32[16,64,256]{2,0,1:T(8,128)}), f32[16,64,256]{2,0,1:T(8,128)S(1)}, u32[]{:S(2)}, u32[]{:S(2)}) %all-to-all-start.4) | async-done | bytes 1048608 | tf_op jit(solution)/shard_map/all_to_all | solution.py:116
  368.2 1.6 copy.113
  (283 shorter events, 84.1 us)
Async XLA Ops:
  0.6 139.3 %copy-start = (bf16[256,160]{0,1:T(8,128)(2,1)S(1)}, bf16[256,160]{0,1:T(8,128)(2,1)}, u32[]{:S(2)}) copy-start(bf16[256,160]{0,1:T(8,128)(2,1)} %param.24) | copy-start | bytes 245764
  0.6 20.3 %copy-start.3 = (f32[8,16,2048]{2,1,0:T(8,128)S(1)}, f32[8,16,2048]{2,1,0:T(8,128)}, u32[]{:S(2)}) copy-start(f32[8,16,2048]{2,1,0:T(8,128)} %param.30) | copy-start | bytes 3145732
  8.6 17.1 %copy-start.2 = (bf16[8,16,1024]{2,1,0:T(8,128)(2,1)S(1)}, bf16[8,16,1024]{2,1,0:T(8,128)(2,1)}, u32[]{:S(2)}) copy-start(bf16[8,16,1024]{2,1,0:T(8,128)(2,1)} %param.19) | copy-start | bytes 786436
  8.6 17.4 %copy-start.4 = (f32[1024]{0:T(1024)S(1)}, f32[1024]{0:T(1024)}, u32[]{:S(2)}) copy-start(f32[1024]{0:T(1024)} %param.20) | copy-start | bytes 12292
  13.7 47.4 %all-to-all-start.1 = ((f32[8,1,6144]{2,1,0:T(1,128)}), f32[8,1,6144]{2,1,0:T(1,128)S(1)}, u32[]{:S(2)}, u32[]{:S(2)}) async-start(f32[8,1,6144]{2,1,0:T(1,128)} %reshape.188), calls=%async_computation.1 | async-start | bytes 393216 | tf_op jit(solution)/shard_map/all_to_all | solution.py:44
  52.9 8.2 %copy-start.12 = (s32[64]{0:T(128)S(1)}, s32[64]{0:T(128)}, u32[]{:S(2)}) copy-start(s32[64]{0:T(128)} %param.33) | copy-start | bytes 772
  52.9 14.3 %copy-start.13 = (s32[64]{0:T(128)S(1)}, s32[64]{0:T(128)}, u32[]{:S(2)}) copy-start(s32[64]{0:T(128)} %param.32) | copy-start | bytes 772
  52.9 25.7 %copy-start.9 = (s32[64]{0:T(128)S(1)}, s32[64]{0:T(128)}, u32[]{:S(2)}) copy-start(s32[64]{0:T(128)} %param.35) | copy-start | bytes 772
  52.9 25.9 %copy-start.6 = (f32[4,256]{1,0:T(4,128)S(1)}, f32[4,256]{1,0:T(4,128)}, u32[]{:S(2)}) copy-start(f32[4,256]{1,0:T(4,128)} %param.22) | copy-start | bytes 12292
  52.9 25.9 %copy-start.5 = (f32[16,256]{1,0:T(8,128)S(1)}, f32[16,256]{1,0:T(8,128)}, u32[]{:S(2)}) copy-start(f32[16,256]{1,0:T(8,128)} %param.27) | copy-start | bytes 49156
  61.1 31.4 %all-to-all-start = ((f32[8,1,32768]{2,1,0:T(1,128)}), f32[8,1,32768]{2,1,0:T(1,128)S(1)}, u32[]{:S(2)}, u32[]{:S(2)}) async-start(f32[8,1,32768]{2,1,0:T(1,128)} %reshape.184), calls=%async_computation | async-start | bytes 2097152 | tf_op jit(solution)/shard_map/all_to_all | solution.py:43
  92.5 29.4 %all-to-all-start.2 = ((bf16[8,2,32768]{2,1,0:T(2,128)(2,1)}), bf16[8,2,32768]{2,1,0:T(2,128)(2,1)S(1)}, u32[]{:S(2)}, u32[]{:S(2)}) async-start(bf16[8,2,32768]{2,1,0:T(2,128)(2,1)} %reshape.186), calls=%async_computation.2 | async-start | bytes 2097152 | tf_op jit(solution)/shard_map/all_to_all | solution.py:50
  112.4 27.0 %copy-start.7 = (f32[256]{0:T(256)S(1)}, f32[256]{0:T(256)}, u32[]{:S(2)}) copy-start(f32[256]{0:T(256)} %param.23) | copy-start | bytes 3076
  129.5 55.2 %copy-start.10 = (bf16[128,256]{1,0:T(8,128)(2,1)S(1)}, bf16[128,256]{1,0:T(8,128)(2,1)}, u32[]{:S(2)}) copy-start(bf16[128,256]{1,0:T(8,128)(2,1)} %param.25) | copy-start | bytes 196612
  129.5 55.2 %copy-start.11 = (f32[256]{0:T(256)S(1)}, f32[256]{0:T(256)}, u32[]{:S(2)}) copy-start(f32[256]{0:T(256)} %param.26) | copy-start | bytes 3076
  138.4 1.0 copy-start.1
  138.4 52.8 %copy-start.14 = (s32[64]{0:T(128)S(1)}, s32[64]{0:T(128)}, u32[]{:S(2)}) copy-start(s32[64]{0:T(128)} %param.34) | copy-start | bytes 772
  191.2 134.3 %copy-start.8 = (f32[256]{0:T(256)S(1)}, f32[256]{0:T(256)}, u32[]{:S(2)}) copy-start(f32[256]{0:T(256)} %param.28) | copy-start | bytes 3076
  328.1 14.0 %all-to-all-start.3 = ((bf16[16,64,256]{2,0,1:T(8,128)(2,1)}), bf16[16,64,256]{2,0,1:T(8,128)(2,1)S(1)}, u32[]{:S(2)}, u32[]{:S(2)}) async-start(bf16[16,64,256]{2,0,1:T(8,128)(2,1)} %copy.108), calls=%async_computation.3 | async-start | bytes 1048576 | tf_op jit(solution)/shard_map/all_to_all | solution.py:109
  342.1 25.5 %all-to-all-start.4 = ((f32[16,64,256]{2,0,1:T(8,128)}), f32[16,64,256]{2,0,1:T(8,128)S(1)}, u32[]{:S(2)}, u32[]{:S(2)}) async-start(f32[16,64,256]{2,0,1:T(8,128)} %bitcast.121), calls=%async_computation.4 | async-start | bytes 2097152 | tf_op jit(solution)/shard_map/all_to_all | solution.py:116
where the time goes:
time: 372 us; the launch traced here: 370 us
  local copies, waits for them, and re-layouts  191 us (51%)
  other arithmetic  47.8 us (13%)
  blocking collectives  43.6 us (12%)
  waiting for transfers between devices  33.9 us (9%)
  starting transfers between devices  29.5 us (8%)
  loops' own time  12.3 us (3%)
  matrix products  10.8 us (3%)
    unnamed x47, local copies, waits for them, and re-layouts  70.4 us
    psum x1, blocking collectives, on_device(): mixed_rows = lax.psum(partial_value, 'req').astype(jnp.bfloat16)  43.6 us
    dynamic_update_slice x16, local copies, waits for them, and re-layouts, on_device(): lax.scan(advance, (start_flat, start_flat), sliced)  31.1 us
    while x48, local copies, waits for them, and re-layouts  29.4 us
    dynamic_slice x16, other arithmetic, on_device(): lax.scan(advance, (start_flat, start_flat), sliced)  20.9 us
    reduce_sum x16, other arithmetic, advance(): result = jnp.sum(spread(step_c) * current, axis=0)  14.9 us
    another operation x1, loops' own time, on_device(): lax.scan(advance, (start_flat, start_flat), sliced)  12.3 us
    all_to_all x1, waiting for transfers between devices, on_device(): lax.all_to_all(chosen.reshape(state_size, all_reqs, channels), 'req', spl...  12.2 us
  transfers between devices with their start and end apart: 5, of which 4 were waited for; matrix products, arithmetic and copies ran while one was open for 23% of the time, Pallas kernels for 0%

commit v1 on v0

--- a/solution.py
+++ b/solution.py
@@ -4,6 +4,17 @@
 from jax.sharding import PartitionSpec as P
 
 EPS = 1e-05
+
+
+def split_up(x, dim, size):
+    before, after = (x.shape[:dim], x.shape[dim + 1 :])
+    return jnp.moveaxis(x.reshape(*before, size, -1, *after), dim, 0)
+
+
+def joined_along(blocks, dim):
+    blocks = jnp.moveaxis(blocks, 0, dim)
+    shape = blocks.shape
+    return blocks.reshape(*shape[:dim], shape[dim] * shape[dim + 1], *shape[dim + 2 :])
 
 
 def rms_normed(values_in, norm_gain):
@@ -47,7 +58,15 @@
     normed = rms_normed(token_major, norm_gain)
     projected = jnp.dot(normed, in_weight, preferred_element_type=jnp.float32).astype(jnp.bfloat16)
     projected = jnp.moveaxis(projected.reshape(draft_len, local_reqs, 2, inner_width), 2, 0)
-    grouped = lax.all_to_all(projected, "req", split_axis=3, concat_axis=2, tiled=True)
+    peers, place = (lax.axis_size("req"), lax.axis_index("req"))
+    blocks = split_up(projected, 3, peers)
+    filled = blocks
+    for step in range(1, peers):
+        target, source = ((place + step) % peers, (place - step) % peers)
+        sent = lax.dynamic_index_in_dim(blocks, target, 0)
+        received = lax.ppermute(sent, "req", [(i, (i + step) % peers) for i in range(peers)])
+        filled = lax.dynamic_update_slice_in_dim(filled, received, source, axis=0)
+    grouped = joined_along(filled, 2)
     all_reqs = grouped.shape[2]
     inner_part = grouped[0]
     gate_part = grouped[1]

time: 372 us -> 326 us (0.88)
  local copies, waits for them, and re-layouts: 191 us -> 146 us
  waiting for transfers between devices: 33.9 us -> 23.1 us
  starting transfers between devices: 29.5 us -> 37.5 us
    unnamed x47 -> x44, local copies, waits for them, and re-layouts: 70.4 us -> 43 us
    ppermute x0 -> x7, starting transfers between devices: none -> 16.4 us  [on_device(): lax.ppermute(sent, 'req', [(i, (i + step) % peers) for i in range(peers)])]
    all_to_all x1 -> x0, waiting for transfers between devices: 9.5 us -> none  [on_device(): lax.all_to_all(projected, 'req', split_axis=3, concat_axis=2, tiled=True)]
    all_to_all x1 -> x0, local copies, waits for them, and re-layouts: 8.9 us -> none  [on_device(): lax.all_to_all(projected, 'req', split_axis=3, concat_axis=2, tiled=True)]
    reshape x1, local copies, waits for them, and re-layouts: 8.85 us -> 0.1 us  [split_up(): return jnp.moveaxis(x.reshape(*before, size, -1, *after), dim, 0)]
    all_to_all x1, starting transfers between devices: 7.25 us -> 3.39 us  [on_device(): lax.all_to_all(edge_lead, 'req', split_axis=2, concat_axis=1, tiled=True)]
    all_to_all x1 -> x0, starting transfers between devices: 3.74 us -> none  [on_device(): lax.all_to_all(projected, 'req', split_axis=3, concat_axis=2, tiled=True)]
  transfers between devices with their start and end apart: 5 -> 11, of which waited for: 4 -> 3; matrix products, arithmetic and copies ran while one was open for 23% -> 17% of each run, Pallas kernels for 0% -> 0%
where the time goes in v1:
time: 326 us; the launch traced here: 325 us
  local copies, waits for them, and re-layouts  146 us (45%)
  other arithmetic  49.2 us (15%)
  blocking collectives  46.1 us (14%)
  starting transfers between devices  37.5 us (12%)
  waiting for transfers between devices  23.1 us (7%)
  loops' own time  11.8 us (4%)
  matrix products  9.02 us (3%)
    psum x1, blocking collectives, on_device(): mixed_rows = lax.psum(partial_value, 'req').astype(jnp.bfloat16)  46.1 us
    unnamed x44, local copies, waits for them, and re-layouts  43 us
    dynamic_update_slice x16, local copies, waits for them, and re-layouts, on_device(): lax.scan(advance, (start_flat, start_flat), sliced)  31.1 us
    while x48, local copies, waits for them, and re-layouts  29.4 us
    dynamic_slice x16, other arithmetic, on_device(): lax.scan(advance, (start_flat, start_flat), sliced)  20.9 us
    ppermute x7, starting transfers between devices, on_device(): lax.ppermute(sent, 'req', [(i, (i + step) % peers) for i in range(peers)])  16.4 us
    reduce_sum x16, other arithmetic, advance(): result = jnp.sum(spread(step_c) * current, axis=0)  14.9 us
    all_to_all x1, waiting for transfers between devices, on_device(): lax.all_to_all(chosen.reshape(state_size, all_reqs, channels), 'req', spl...  12.1 us
  transfers between devices with their start and end apart: 11, of which 3 were waited for; matrix products, arithmetic and copies ran while one was open for 17% of the time, Pallas kernels for 0%

profile of v1, /device:TPU:0, one launch (start us, length us, event | category | flops | bytes accessed | tf_op | source)
XLA Modules:
  0.0 324.6 jit_solution(671944238314011705)
XLA Ops:
  2.1 4.9 %convolution_convert_fusion = bf16[128,4096]{1,0:T(8,128)(2,1)S(1)} fusion(bf16[1024,4096]{1,0:T(8,128)(2,1)} %param.21, f32[1024]{0:T(1024)} %param.20, f32[128]{0:T(128)S(1)} %rsqrt.12, bf16[8,16,1024]{2,1,0:T(8,128)(2,1)} %param.19), kind=kOutput, calls=%fused_computation.11 | convolution fusion | flops 1074790400 | bytes 9703936 | tf_op jit(solution)/shard_map/dot_general | solution.py:59
  7.8 2.9 collective-permute-start
  11.4 1.6 collective-permute-start.1
  13.0 2.6 collective-permute-start.2
  16.9 2.7 collective-permute-start.4
  19.6 2.7 copy.92
  22.3 3.9 %bitcast_bitcast_fusion.1 = f32[2048,3,8]{2,1,0:T(4,128)} fusion(f32[8,3,2048]{0,1,2:T(4,128)} %copy.92), kind=kLoop, calls=%fused_computation.93 | loop fusion | bytes 393216
  26.2 5.2 %reshape.198 = f32[8,1,6144]{2,1,0:T(1,128)} reshape(f32[2048,3,8]{2,1,0:T(4,128)} %bitcast_bitcast_fusion.1) | data formatting | bytes 393216
  31.4 3.4 %all-to-all-start.1 = ((f32[8,1,6144]{2,1,0:T(1,128)}), f32[8,1,6144]{2,1,0:T(1,128)S(1)}, u32[]{:S(2)}, u32[]{:S(2)}) async-start(f32[8,1,6144]{2,1,0:T(1,128)} %reshape.198), calls=%async_computation.1 | async-start | bytes 393216 | tf_op jit(solution)/shard_map/all_to_all | solution.py:55
  34.8 4.6 %copy.86 = f32[8,16,2048]{1,0,2:T(8,128)} copy(f32[8,16,2048]{2,1,0:T(8,128)S(1)} %copy-done.3) | data formatting | bytes 2097152 | tf_op args[11]
  39.5 5.8 %bitcast_bitcast_fusion = f32[2048,8,16]{2,1,0:T(8,128)} fusion(f32[8,16,2048]{1,0,2:T(8,128)} %copy.86), kind=kLoop, calls=%fused_computation.92 | loop fusion | bytes 2097152
  45.8 8.1 %reshape.196 = f32[8,1,32768]{2,1,0:T(1,128)} reshape(f32[2048,8,16]{2,1,0:T(8,128)} %bitcast_bitcast_fusion) | data formatting | bytes 2097152
  54.2 3.8 %collective-permute-start.5 = (bf16[1,2,16,8,256]{4,3,0,2,1:T(8,128)(2,1)S(1)}, bf16[1,2,16,8,256]{4,3,0,2,1:T(8,128)(2,1)S(1)}, u32[]{:S(2)}, u32[]{:S(2)}) collective-permute-start(bf16[1,2,16,8,256]{4,3,0,2,1:T(8,128)(2,1)S(1)} %bitcast.207), channel_id=1, source_target_pairs={{0,24},{4,28},{8,0},{12,4},{16,8},{20,12},{24,16},{28,20},{1,25},{... | collective-permute-start | bytes 393224 | tf_op jit(solution)/shard_map/ppermute | solution.py:67
  58.9 1.5 collective-permute-start.6
  62.4 1.6 collective-permute-done.6
  64.1 5.4 %all-to-all-start = ((f32[8,1,32768]{2,1,0:T(1,128)}), f32[8,1,32768]{2,1,0:T(1,128)}, u32[]{:S(2)}, u32[]{:S(2)}) async-start(f32[8,1,32768]{2,1,0:T(1,128)} %reshape.196), calls=%async_computation | async-start | bytes 2097152 | tf_op jit(solution)/shard_map/all_to_all | solution.py:54
  71.2 4.7 %reshape.199 = f32[2048,3,8]{2,1,0:T(4,128)} reshape(f32[8,6144]{1,0:T(8,128)S(1)} %reduce.3) | data formatting | bytes 393216
  75.8 3.5 %copy.93 = f32[3,8,8,256]{3,0,1,2:T(4,128)S(1)} copy(f32[3,8,8,256]{1,0,3,2:T(4,128)} %bitcast.178) | data formatting | bytes 393216 | tf_op jit(solution)/shard_map/all_to_all | solution.py:55
  81.1 46.1 %all-reduce.1 = bf16[1024,160]{0,1:T(8,128)(2,1)S(1)} all-reduce(f32[1024,160]{0,1:T(8,128)S(1)} %fusion.29), channel_id=1, replica_groups=mesh['req'=8,'grp'=4] {'req'}, use_global_device_ids=true, to_apply=%region_1.2 | all-reduce | flops 163840 | bytes 983040 | tf_op jit(solution)/shard_map/psum | solution.py:86
  129.2 1.3 copy.124
  130.7 4.4 %reduce.2 = f32[8,32768]{1,0:T(8,128)S(1)} reduce(f32[8,1,32768]{2,1,0:T(1,128)} %all-to-all-done, f32[]{:T(128)} %broadcast.103), dimensions={1}, to_apply=%all_to_all.50.reduce_sub_computation | reduce | bytes 2097156 | tf_op jit(solution)/shard_map/all_to_all | solution.py:54
  135.0 6.0 %reshape.197 = f32[2048,8,16]{2,1,0:T(8,128)} reshape(f32[8,32768]{1,0:T(8,128)S(1)} %reduce.2) | data formatting | bytes 2097152
  141.0 5.4 %copy.88 = f32[16,8,8,256]{3,2,1,0:T(8,128)S(1)} copy(f32[16,8,8,256]{0,2,3,1:T(8,128)} %bitcast.177) | data formatting | bytes 2097152 | tf_op jit(solution)/shard_map/all_to_all | solution.py:54
  148.0 131.0 %while.15 = (s32[]{:T(128)}, f32[16,16384]{1,0:T(8,128)S(1)}, f32[16,16384]{1,0:T(8,128)S(1)}, f32[16,16384]{1,0:T(8,128)}, f32[16,16384]{1,0:T(8,128)}, /*index...) while((s32[]{:T(128)}, f32[16,16384]{1,0:T(8,128)S(1)}, ...), condition=%wide.region_4.5_spmd.clone, body=%wide.region_2.4_spmd.clone.sunk | while | flops 1835075 | bytes 18522676 | solution.py:123
  149.9 1.3 constant_dynamic-slice_fusion.13
  154.5 1.9 dynamic_update_slice.41
  158.1 1.3 constant_dynamic-slice_fusion.13
  162.7 1.9 dynamic_update_slice.41
  166.3 1.3 constant_dynamic-slice_fusion.13
  170.8 1.9 dynamic_update_slice.41
  174.4 1.3 constant_dynamic-slice_fusion.13
  179.0 1.9 dynamic_update_slice.41
  182.6 1.3 constant_dynamic-slice_fusion.13
  187.1 1.9 dynamic_update_slice.41
  190.7 1.3 constant_dynamic-slice_fusion.13
  195.3 1.9 dynamic_update_slice.41
  198.9 1.3 constant_dynamic-slice_fusion.13
  203.5 1.9 dynamic_update_slice.41
  207.1 1.3 constant_dynamic-slice_fusion.13
  211.6 1.9 dynamic_update_slice.41
  215.2 1.3 constant_dynamic-slice_fusion.13
  219.8 1.9 dynamic_update_slice.41
  223.4 1.3 constant_dynamic-slice_fusion.13
  228.0 1.9 dynamic_update_slice.41
  231.6 1.3 constant_dynamic-slice_fusion.13
  236.2 1.9 dynamic_update_slice.41
  239.8 1.3 constant_dynamic-slice_fusion.13
  244.3 1.9 dynamic_update_slice.41
  247.9 1.3 constant_dynamic-slice_fusion.13
  252.5 1.9 dynamic_update_slice.41
  256.1 1.3 constant_dynamic-slice_fusion.13
  260.7 1.9 dynamic_update_slice.41
  264.3 1.3 constant_dynamic-slice_fusion.13
  268.9 1.9 dynamic_update_slice.41
  272.5 1.3 constant_dynamic-slice_fusion.13
  277.0 1.9 dynamic_update_slice.41
  279.0 1.5 copy.125
  280.5 1.5 fusion.16
  283.1 3.5 %all-to-all-start.2 = ((bf16[16,64,256]{2,0,1:T(8,128)(2,1)}), bf16[16,64,256]{2,0,1:T(8,128)(2,1)S(1)}, u32[]{:S(2)}, u32[]{:S(2)}) async-start(bf16[16,64,256]{2,0,1:T(8,128)(2,1)} %copy.106), calls=%async_computation.2 | async-start | bytes 1048576 | tf_op jit(solution)/shard_map/all_to_all | solution.py:128
  287.8 9.4 %all-to-all-done.2 = bf16[16,64,256]{2,0,1:T(8,128)(2,1)S(1)} async-done(((bf16[16,64,256]{2,0,1:T(8,128)(2,1)}), bf16[16,64,256]{2,0,1:T(8,128)(2,1)S(1)}, u32[]{:S(2)}, u32[]{:S(2)}) %all-to-all-start.2) | async-done | bytes 524320 | tf_op jit(solution)/shard_map/all_to_all | solution.py:128
  297.2 8.8 %all-to-all-start.3 = ((f32[16,64,256]{2,0,1:T(8,128)}), f32[16,64,256]{2,0,1:T(8,128)S(1)}, u32[]{:S(2)}, u32[]{:S(2)}) async-start(f32[16,64,256]{2,0,1:T(8,128)} %bitcast.135), calls=%async_computation.3 | async-start | bytes 2097152 | tf_op jit(solution)/shard_map/all_to_all | solution.py:135
  306.4 3.0 fusion.2
  310.3 12.1 %all-to-all-done.3 = f32[16,64,256]{2,0,1:T(8,128)S(1)} async-done(((f32[16,64,256]{2,0,1:T(8,128)}), f32[16,64,256]{2,0,1:T(8,128)S(1)}, u32[]{:S(2)}, u32[]{:S(2)}) %all-to-all-start.3) | async-done | bytes 1048608 | tf_op jit(solution)/shard_map/all_to_all | solution.py:135
  323.0 1.6 copy.111
  (305 shorter events, 85.9 us)
Async XLA Ops:
  0.6 80.2 %copy-start = (bf16[256,160]{0,1:T(8,128)(2,1)S(1)}, bf16[256,160]{0,1:T(8,128)(2,1)}, u32[]{:S(2)}) copy-start(bf16[256,160]{0,1:T(8,128)(2,1)} %param.24) | copy-start | bytes 245764
  2.0 17.6 %copy-start.4 = (bf16[8,3,2048]{2,0,1:T(8,128)(2,1)S(1)}, bf16[8,3,2048]{2,0,1:T(8,128)(2,1)}, u32[]{:S(2)}) copy-start(bf16[8,3,2048]{2,0,1:T(8,128)(2,1)} %param.31) | copy-start | bytes 294916
  7.8 46.4 %collective-permute-start = (bf16[1,2,16,8,256]{4,3,0,2,1:T(8,128)(2,1)}, bf16[1,2,16,8,256]{4,3,0,2,1:T(8,128)(2,1)}, u32[]{:S(2)}, u32[]{:S(2)}) collective-permute-start(bf16[1,2,16,8,256]{4,3,0,2,1:T(8,128)(2,1)} %bitcast.145), channel_id=1, source_target_pairs={{0,4},{4,8},{8,12},{12,16},{16,20},{20,24},{24,28},{28,0},{1,5},{5... | collective-permute-start | bytes 393224 | tf_op jit(solution)/shard_map/ppermute | solution.py:67
  11.4 47.5 %collective-permute-start.1 = (bf16[1,2,16,8,256]{4,3,0,2,1:T(8,128)(2,1)}, bf16[1,2,16,8,256]{4,3,0,2,1:T(8,128)(2,1)}, u32[]{:S(2)}, u32[]{:S(2)}) collective-permute-start(bf16[1,2,16,8,256]{4,3,0,2,1:T(8,128)(2,1)} %bitcast.144), channel_id=1, source_target_pairs={{0,8},{4,12},{8,16},{12,20},{16,24},{20,28},{24,0},{28,4},{1,9},{5... | collective-permute-start | bytes 393224 | tf_op jit(solution)/shard_map/ppermute | solution.py:67
  13.0 48.4 %collective-permute-start.2 = (bf16[1,2,16,8,256]{4,3,0,2,1:T(8,128)(2,1)S(1)}, bf16[1,2,16,8,256]{4,3,0,2,1:T(8,128)(2,1)}, u32[]{:S(2)}, u32[]{:S(2)}) collective-permute-start(bf16[1,2,16,8,256]{4,3,0,2,1:T(8,128)(2,1)S(1)} %bitcast.205), channel_id=1, source_target_pairs={{0,12},{4,16},{8,20},{12,24},{16,28},{20,0},{24,4},{28,8},{1,13},{... | collective-permute-start | bytes 393224 | tf_op jit(solution)/shard_map/ppermute | solution.py:67
  15.6 46.7 %collective-permute-start.3 = (bf16[1,2,16,8,256]{4,3,0,2,1:T(8,128)(2,1)S(1)}, bf16[1,2,16,8,256]{4,3,0,2,1:T(8,128)(2,1)S(1)}, u32[]{:S(2)}, u32[]{:S(2)}) collective-permute-start(bf16[1,2,16,8,256]{4,3,0,2,1:T(8,128)(2,1)S(1)} %bitcast.204), channel_id=1, source_target_pairs={{0,16},{4,20},{8,24},{12,28},{16,0},{20,4},{24,8},{28,12},{1,17},{... | collective-permute-start | bytes 393224 | tf_op jit(solution)/shard_map/ppermute | solution.py:67
  16.9 45.4 %collective-permute-start.4 = (bf16[1,2,16,8,256]{4,3,0,2,1:T(8,128)(2,1)S(1)}, bf16[1,2,16,8,256]{4,3,0,2,1:T(8,128)(2,1)S(1)}, u32[]{:S(2)}, u32[]{:S(2)}) collective-permute-start(bf16[1,2,16,8,256]{4,3,0,2,1:T(8,128)(2,1)S(1)} %bitcast.203), channel_id=1, source_target_pairs={{0,20},{4,24},{8,28},{12,0},{16,4},{20,8},{24,12},{28,16},{1,21},{... | collective-permute-start | bytes 393224 | tf_op jit(solution)/shard_map/ppermute | solution.py:67
  26.2 8.6 %copy-start.3 = (f32[8,16,2048]{2,1,0:T(8,128)S(1)}, f32[8,16,2048]{2,1,0:T(8,128)}, u32[]{:S(2)}) copy-start(f32[8,16,2048]{2,1,0:T(8,128)} %param.30) | copy-start | bytes 3145732
  31.4 32.7 %all-to-all-start.1 = ((f32[8,1,6144]{2,1,0:T(1,128)}), f32[8,1,6144]{2,1,0:T(1,128)S(1)}, u32[]{:S(2)}, u32[]{:S(2)}) async-start(f32[8,1,6144]{2,1,0:T(1,128)} %reshape.198), calls=%async_computation.1 | async-start | bytes 393216 | tf_op jit(solution)/shard_map/all_to_all | solution.py:55
  39.5 5.8 %copy-start.9 = (s32[64]{0:T(128)S(1)}, s32[64]{0:T(128)}, u32[]{:S(2)}) copy-start(s32[64]{0:T(128)} %param.33) | copy-start | bytes 772
  39.5 5.9 %copy-start.11 = (s32[64]{0:T(128)S(1)}, s32[64]{0:T(128)}, u32[]{:S(2)}) copy-start(s32[64]{0:T(128)} %param.32) | copy-start | bytes 772
  39.5 5.9 %copy-start.6 = (f32[4,256]{1,0:T(4,128)S(1)}, f32[4,256]{1,0:T(4,128)}, u32[]{:S(2)}) copy-start(f32[4,256]{1,0:T(4,128)} %param.22) | copy-start | bytes 12292
  39.5 5.9 %copy-start.5 = (f32[16,256]{1,0:T(8,128)S(1)}, f32[16,256]{1,0:T(8,128)}, u32[]{:S(2)}) copy-start(f32[16,256]{1,0:T(8,128)} %param.27) | copy-start | bytes 49156
  39.5 6.0 %copy-start.10 = (s32[64]{0:T(128)S(1)}, s32[64]{0:T(128)}, u32[]{:S(2)}) copy-start(s32[64]{0:T(128)} %param.35) | copy-start | bytes 772
  54.2 8.1 %collective-permute-start.5 = (bf16[1,2,16,8,256]{4,3,0,2,1:T(8,128)(2,1)S(1)}, bf16[1,2,16,8,256]{4,3,0,2,1:T(8,128)(2,1)S(1)}, u32[]{:S(2)}, u32[]{:S(2)}) collective-permute-start(bf16[1,2,16,8,256]{4,3,0,2,1:T(8,128)(2,1)S(1)} %bitcast.207), channel_id=1, source_target_pairs={{0,24},{4,28},{8,0},{12,4},{16,8},{20,12},{24,16},{28,20},{1,25},{... | collective-permute-start | bytes 393224 | tf_op jit(solution)/shard_map/ppermute | solution.py:67
  58.9 5.0 %collective-permute-start.6 = (bf16[1,2,16,8,256]{4,3,0,2,1:T(8,128)(2,1)S(1)}, bf16[1,2,16,8,256]{4,3,0,2,1:T(8,128)(2,1)S(1)}, u32[]{:S(2)}, u32[]{:S(2)}) collective-permute-start(bf16[1,2,16,8,256]{4,3,0,2,1:T(8,128)(2,1)S(1)} %bitcast.206), channel_id=1, source_target_pairs={{0,28},{4,0},{8,4},{12,8},{16,12},{20,16},{24,20},{28,24},{1,29},{... | collective-permute-start | bytes 393224 | tf_op jit(solution)/shard_map/ppermute | solution.py:67
  64.0 11.9 %copy-start.2 = (bf16[8,2,16,8,256]{4,3,0,2,1:T(8,128)(2,1)}, bf16[8,2,16,8,256]{4,3,0,2,1:T(8,128)(2,1)S(1)}, u32[]{:S(2)}) copy-start(bf16[8,2,16,8,256]{4,3,0,2,1:T(8,128)(2,1)S(1)} %constant_dynamic-update-slice_fusion) | copy-start | bytes 3145732
  64.1 66.5 %all-to-all-start = ((f32[8,1,32768]{2,1,0:T(1,128)}), f32[8,1,32768]{2,1,0:T(1,128)}, u32[]{:S(2)}, u32[]{:S(2)}) async-start(f32[8,1,32768]{2,1,0:T(1,128)} %reshape.196), calls=%async_computation | async-start | bytes 2097152 | tf_op jit(solution)/shard_map/all_to_all | solution.py:54
  71.2 9.2 %copy-start.7 = (f32[256]{0:T(256)S(1)}, f32[256]{0:T(256)}, u32[]{:S(2)}) copy-start(f32[256]{0:T(256)} %param.23) | copy-start | bytes 3076
  75.8 51.4 %copy-start.12 = (bf16[128,256]{1,0:T(8,128)(2,1)S(1)}, bf16[128,256]{1,0:T(8,128)(2,1)}, u32[]{:S(2)}) copy-start(bf16[128,256]{1,0:T(8,128)(2,1)} %param.25) | copy-start | bytes 196612
  75.8 51.4 %copy-start.13 = (f32[256]{0:T(256)S(1)}, f32[256]{0:T(256)}, u32[]{:S(2)}) copy-start(f32[256]{0:T(256)} %param.26) | copy-start | bytes 3076
  147.0 1.0 copy-start.14
  148.0 132.5 %copy-start.8 = (f32[256]{0:T(256)S(1)}, f32[256]{0:T(256)}, u32[]{:S(2)}) copy-start(f32[256]{0:T(256)} %param.28) | copy-start | bytes 3076
  283.1 14.0 %all-to-all-start.2 = ((bf16[16,64,256]{2,0,1:T(8,128)(2,1)}), bf16[16,64,256]{2,0,1:T(8,128)(2,1)S(1)}, u32[]{:S(2)}, u32[]{:S(2)}) async-start(bf16[16,64,256]{2,0,1:T(8,128)(2,1)} %copy.106), calls=%async_computation.2 | async-start | bytes 1048576 | tf_op jit(solution)/shard_map/all_to_all | solution.py:128
  297.2 25.2 %all-to-all-start.3 = ((f32[16,64,256]{2,0,1:T(8,128)}), f32[16,64,256]{2,0,1:T(8,128)S(1)}, u32[]{:S(2)}, u32[]{:S(2)}) async-start(f32[16,64,256]{2,0,1:T(8,128)} %bitcast.135), calls=%async_computation.3 | async-start | bytes 2097152 | tf_op jit(solution)/shard_map/all_to_all | solution.py:135
  306.4 18.2 %copy-start.1 = (bf16[256,160]{0,1:T(8,128)(2,1)S(1)}, bf16[256,160]{0,1:T(8,128)(2,1)}, u32[]{:S(2)}) copy-start(bf16[256,160]{0,1:T(8,128)(2,1)} %param.24) | copy-start | bytes 245764
